TPU v7x, 32 devices: a whole 2x2x4 slice. The times are simulated.
32 devices in a mesh: slab: 8 (over y, x, core), grp: 4 (over z).
Axes of the slice: x: 2, y: 2, z: 4, core: 2. Of those that a mesh axis runs over, the one named last changes fastest.
Arguments:
- volume: float32 [64, 32, 16, 128], P(None, 'slab', 'grp'), may hold values from -6 to 6
- conv_fine: float32 [3, 3, 3, 64, 64], replicated, may hold values from -0.15625 to 0.15625
- down_first: float32 [2, 2, 2, 64, 128], replicated, may hold values from -0.25 to 0.25
- conv_middle: float32 [3, 3, 3, 128, 128], replicated, may hold values from -0.109375 to 0.109375
- down_second: float32 [2, 2, 2, 128, 256], P(None, None, None, None, 'grp'), may hold values from -0.1875 to 0.1875
- conv_coarse: float32 [3, 3, 3, 256, 512], P(None, None, None, None, 'grp'), may hold values from -0.078125 to 0.078125
Outputs:
- features: float32 [512, 8, 128], P('grp', 'slab')
All inputs are finite; a program needn't handle non-finite values.
Results may differ from a plain program's by a relative error of at most 0.000082.
Values sent between devices are 32-bit elements; how exact they have to be, the bound alone decides.
A program may use at most 64 MiB of HBM per device.

v0:
```python
import jax
import jax.numpy as jnp
from jax import lax
from jax.sharding import PartitionSpec as P


def padded_2(cells, sides, width):
    for axis, dim in sides:
        count = lax.axis_size(axis)
        ends = count - 1
        head = lax.slice_in_dim(cells, 0, width, axis=dim)
        tail = lax.slice_in_dim(cells, cells.shape[dim] - width, cells.shape[dim], axis=dim)
        cells = jnp.concatenate(
            [
                lax.ppermute(tail, axis, [(i, (i + 1) % count) for i in range(ends)]),
                cells,
                lax.ppermute(head, axis, [((i + 1) % count, i) for i in range(ends)]),
            ],
            axis=dim,
        )
    return cells


def from_behind(shard, axis, by):
    peers = lax.axis_size(axis)
    pairs = [(i, i + by) for i in range(peers) if 0 <= i + by < peers]
    return lax.ppermute(shard, axis, pairs)


def convolve(field, kernel, stride, padding):
    return lax.conv_general_dilated(
        field[None],
        kernel,
        (stride, stride, stride),
        padding,
        dimension_numbers=("NCDHW", "DHWIO", "NCDHW"),
        precision=lax.Precision.HIGH,
    )[0]


def per_device(volume, conv_fine, down_first, conv_middle, down_second, conv_coarse):
    valid = ((0, 0), (0, 0), (0, 0))
    sideways = ((0, 0), (0, 0), (1, 1))
    padded = padded_2(volume, (("slab", 1), ("grp", 2)), 1)
    level_one = jax.nn.gelu(convolve(padded, conv_fine, 1, sideways), approximate=False)
    level_two = convolve(level_one, down_first, 2, valid)
    padded_two = padded_2(level_two, (("slab", 1), ("grp", 2)), 1)
    level_two = jax.nn.gelu(convolve(padded_two, conv_middle, 1, sideways), approximate=False)
    gathered = lax.all_gather(level_two, "grp", axis=2, tiled=True)
    shares = convolve(gathered, down_second, 2, valid)
    coarse = lax.all_gather(shares, "grp", axis=0, tiled=True)
    planar = ((0, 0), (1, 1), (1, 1))
    summed = convolve(coarse, conv_coarse, 1, ((1, 1), (1, 1), (1, 1)))
    upward = convolve(coarse[:, -1:], conv_coarse[0:1], 1, planar)
    downward = convolve(coarse[:, :1], conv_coarse[2:3], 1, planar)
    from_lower = from_behind(upward, "slab", 1)
    from_upper = from_behind(downward, "slab", -1)
    summed = summed.at[:, :1].add(from_lower)
    summed = summed.at[:, -1:].add(from_upper)
    result = jax.nn.gelu(summed, approximate=False)
    return result.reshape(result.shape[0], result.shape[1], result.shape[2] * result.shape[3])


def solution(mesh):
    placed = (
        P(None, "slab", "grp", None),
        P(),
        P(),
        P(),
        P(None, None, None, None, "grp"),
        P(None, None, None, None, "grp"),
    )
    return jax.shard_map(
        per_device, mesh=mesh, in_specs=placed, out_specs=P("grp", "slab", None), check_vma=False
    )
```

profile of v0, /device:TPU:3, one launch (start us, length us, event | category | flops | bytes accessed | tf_op | source)
XLA Modules:
  0.0 111.9 jit_solution(5088710529204012672)
XLA Ops:
  0.0 0.0 copy-start
  0.0 1.1 %fusion.97 = (f32[64,1,4,128]{3,2,1,0:T(4,128)S(1)}, f32[64,1,4,128]{3,2,1,0:T(4,128)S(1)}) fusion(f32[64,4,4,128]{3,2,1,0:T(4,128)} %param.14), kind=kLoop, calls=%fused_computation.132 | loop fusion | bytes 524288 | tf_op jit(solution)/shard_map/slice | solution.py:11
  1.2 3.7 %collective-permute-start = (f32[64,1,4,128]{3,0,2,1:T(8,128)S(1)}, f32[64,1,4,128]{3,0,2,1:T(8,128)S(1)}, u32[]{:S(2)}, u32[]{:S(2)}) collective-permute-start(f32[64,1,4,128]{3,0,2,1:T(8,128)S(1)} %copy.117), channel_id=1, source_target_pairs={{0,4},{4,8},{8,12},{12,16},{16,20},{20,24},{24,28},{1,5},{5,9},{9,... | collective-permute-start | bytes 393224 | tf_op jit(solution)/shard_map/ppermute | solution.py:15
  4.9 1.9 %collective-permute-start.1 = (f32[64,1,4,128]{3,0,2,1:T(8,128)S(1)}, f32[64,1,4,128]{3,0,2,1:T(8,128)S(1)}, u32[]{:S(2)}, u32[]{:S(2)}) collective-permute-start(f32[64,1,4,128]{3,0,2,1:T(8,128)S(1)} %copy.118), channel_id=1, source_target_pairs={{4,0},{8,4},{12,8},{16,12},{20,16},{24,20},{28,24},{5,1},{9,5},{13... | collective-permute-start | bytes 393224 | tf_op jit(solution)/shard_map/ppermute | solution.py:17
  6.8 0.0 collective-permute-done
  6.8 0.0 copy-done.2
  6.8 0.2 constant_dynamic-update-slice_fusion.1
  7.0 5.1 %collective-permute-done.1 = f32[64,1,4,128]{3,0,2,1:T(8,128)S(1)} collective-permute-done((f32[64,1,4,128]{3,0,2,1:T(8,128)S(1)}, f32[64,1,4,128]{3,0,2,1:T(8,128)S(1)}, u32[]{:S(2)}, u32[]{:S(2)}) %collective-permute-start.1) | collective-permute-done | bytes 131104 | tf_op jit(solution)/shard_map/ppermute | solution.py:17
  12.1 3.2 %collective-permute-start.2 = (f32[64,6,1,128]{3,0,2,1:T(8,128)S(1)}, f32[64,6,1,128]{3,0,2,1:T(8,128)S(1)}, u32[]{:S(2)}, u32[]{:S(2)}) collective-permute-start(f32[64,6,1,128]{3,0,2,1:T(8,128)S(1)} %get-tuple-element.45), channel_id=1, source_target_pairs={{0,1},{1,2},{2,3},{4,5},{5,6},{6,7},{8,9},{9,10},{10,11},{12,13},{... | collective-permute-start | bytes 589832 | tf_op jit(solution)/shard_map/ppermute | solution.py:15
  15.3 1.3 %collective-permute-start.3 = (f32[64,6,1,128]{3,0,2,1:T(8,128)S(1)}, f32[64,6,1,128]{3,0,2,1:T(8,128)S(1)}, u32[]{:S(2)}, u32[]{:S(2)}) collective-permute-start(f32[64,6,1,128]{3,0,2,1:T(8,128)S(1)} %get-tuple-element.46), channel_id=1, source_target_pairs={{1,0},{2,1},{3,2},{5,4},{6,5},{7,6},{9,8},{10,9},{11,10},{13,12},{... | collective-permute-start | bytes 589832 | tf_op jit(solution)/shard_map/ppermute | solution.py:17
  16.6 1.7 %collective-permute-done.2 = f32[64,6,1,128]{3,0,2,1:T(8,128)S(1)} collective-permute-done((f32[64,6,1,128]{3,0,2,1:T(8,128)S(1)}, f32[64,6,1,128]{3,0,2,1:T(8,128)S(1)}, u32[]{:S(2)}, u32[]{:S(2)}) %collective-permute-start.2) | collective-permute-done | bytes 196640 | tf_op jit(solution)/shard_map/ppermute | solution.py:15
  18.4 4.1 %collective-permute-done.3 = f32[64,6,1,128]{3,0,2,1:T(8,128)S(1)} collective-permute-done((f32[64,6,1,128]{3,0,2,1:T(8,128)S(1)}, f32[64,6,1,128]{3,0,2,1:T(8,128)S(1)}, u32[]{:S(2)}, u32[]{:S(2)}) %collective-permute-start.3) | collective-permute-done | bytes 196640 | tf_op jit(solution)/shard_map/ppermute | solution.py:17
  22.5 0.1 maximum_bitcast_fusion
  22.6 4.2 %copy.106 = f32[64,6,6,1,128]{0,3,4,2,1:T(1,128)} copy(f32[64,6,6,1,128]{4,0,2,1,3:T(8,128)S(1)} %maximum_bitcast_fusion) | data formatting | bytes 2359296
  26.8 3.4 %pad.6.clone = f32[64,6,6,1,136]{0,3,4,2,1:T(1,128)S(1)} pad(f32[64,6,6,1,128]{0,3,4,2,1:T(1,128)} %copy.106, f32[]{:T(128)} %constant.74.clone.1), padding=0_0x0_0x0_0x0_0x1_7 | pad | bytes 2433028 | tf_op jit(solution)/shard_map/broadcast_in_dim | solution.py:32
  30.2 0.0 copy-start.7
  30.2 0.0 copy-start.8
  30.2 0.2 copy.71
  30.4 0.9 copy-done.7
  31.4 0.0 copy-done.8
  31.4 8.9 %fusion.22 = f32[4,4,8,17,64]{4,2,3,1,0:T(8,128)S(1)} fusion(f32[3,3,3,64,64]{4,3,2,1,0:T(8,128)S(1)} %copy-done.7, f32[64,6,6,1,7,2]{0,4,5,2,1,3:T(8,128)S(1)} %slice.107, f32[64,6,6,1,8,17]{0,4,5,2,1,3:T(8,128)S(1)} %copy.71, pred[8,17]{0,1:T(8,128)(4,1)S(1)} %copy-done.8), kind=kOutput, calls=%fused_computation.21 | convolution fusion | flops 1454131200 | bytes 2381960 | tf_op jit(solution)/shard_map/conv_general_dilated | solution.py:31
  40.3 0.3 copy.72
  40.5 0.1 slice.108
  40.6 0.0 copy-start.4
  40.6 0.8 copy.75
  41.5 0.1 copy-done.4
  41.6 0.6 fusion.24
  42.2 4.2 %collective-permute-start.4 = (f32[128,1,2,64]{0,3,2,1:T(8,128)S(1)}, f32[128,1,2,64]{0,3,2,1:T(8,128)S(1)}, u32[]{:S(2)}, u32[]{:S(2)}) collective-permute-start(f32[128,1,2,64]{0,3,2,1:T(8,128)S(1)} %get-tuple-element.53), channel_id=1, source_target_pairs={{0,4},{4,8},{8,12},{12,16},{16,20},{20,24},{24,28},{1,5},{5,9},{9,... | collective-permute-start | bytes 196616 | tf_op jit(solution)/shard_map/ppermute | solution.py:15
  46.4 1.9 %collective-permute-start.5 = (f32[128,1,2,64]{0,3,2,1:T(8,128)S(1)}, f32[128,1,2,64]{0,3,2,1:T(8,128)S(1)}, u32[]{:S(2)}, u32[]{:S(2)}) collective-permute-start(f32[128,1,2,64]{0,3,2,1:T(8,128)S(1)} %get-tuple-element.54), channel_id=1, source_target_pairs={{4,0},{8,4},{12,8},{16,12},{20,16},{24,20},{28,24},{5,1},{9,5},{13... | collective-permute-start | bytes 196616 | tf_op jit(solution)/shard_map/ppermute | solution.py:17
  48.3 0.0 collective-permute-done.4
  48.3 4.5 %collective-permute-done.5 = f32[128,1,2,64]{0,3,2,1:T(8,128)S(1)} collective-permute-done((f32[128,1,2,64]{0,3,2,1:T(8,128)S(1)}, f32[128,1,2,64]{0,3,2,1:T(8,128)S(1)}, u32[]{:S(2)}, u32[]{:S(2)}) %collective-permute-start.5) | collective-permute-done | bytes 65568 | tf_op jit(solution)/shard_map/ppermute | solution.py:17
  52.9 3.2 %collective-permute-start.6 = (f32[128,4,1,64]{0,3,2,1:T(8,128)S(1)}, f32[128,4,1,64]{0,3,2,1:T(8,128)S(1)}, u32[]{:S(2)}, u32[]{:S(2)}) collective-permute-start(f32[128,4,1,64]{0,3,2,1:T(8,128)S(1)} %get-tuple-element.49), channel_id=1, source_target_pairs={{0,1},{1,2},{2,3},{4,5},{5,6},{6,7},{8,9},{9,10},{10,11},{12,13},{... | collective-permute-start | bytes 393224 | tf_op jit(solution)/shard_map/ppermute | solution.py:15
  56.2 1.3 %collective-permute-start.7 = (f32[128,4,1,64]{0,3,2,1:T(8,128)S(1)}, f32[128,4,1,64]{0,3,2,1:T(8,128)S(1)}, u32[]{:S(2)}, u32[]{:S(2)}) collective-permute-start(f32[128,4,1,64]{0,3,2,1:T(8,128)S(1)} %get-tuple-element.50), channel_id=1, source_target_pairs={{1,0},{2,1},{3,2},{5,4},{6,5},{7,6},{9,8},{10,9},{11,10},{13,12},{... | collective-permute-start | bytes 393224 | tf_op jit(solution)/shard_map/ppermute | solution.py:17
  57.5 0.6 collective-permute-done.6
  58.1 3.8 %collective-permute-done.7 = f32[128,4,1,64]{0,3,2,1:T(8,128)S(1)} collective-permute-done((f32[128,4,1,64]{0,3,2,1:T(8,128)S(1)}, f32[128,4,1,64]{0,3,2,1:T(8,128)S(1)}, u32[]{:S(2)}, u32[]{:S(2)}) %collective-permute-start.7) | collective-permute-done | bytes 131104 | tf_op jit(solution)/shard_map/ppermute | solution.py:17
  61.9 0.3 copy.107
  62.3 0.0 copy-start.6
  62.3 0.1 pad.9.clone
  62.4 0.0 copy-done
  62.5 0.5 copy-done.6
  62.9 1.7 %negate_multiply_fusion.1 = (f32[2,2,8,9,128]{4,2,3,1,0:T(8,128)S(1)}, f32[2,2,8,9,128]{4,2,3,1,0:T(8,128)S(1)}) fusion(f32[3,3,3,128,128]{4,3,2,1,0:T(8,128)S(1)} %copy-done, f32[128,4,4,1,7,2]{0,4,5,2,1,3:T(8,128)S(1)} %slice.114, f32[128,4,4,1,8,9]{0,4,5,2,1,3:T(8,128)S(1)} %copy.79, pred[8,9]{0,1:T(8,128)(4,1)S(1)} %copy-done.6), kind=kOutput, calls=%fused_computation.66 | convolution fusion | flops 765100032 | bytes 2768968 | tf_op jit(solution)/shard_map/conv_general_dilated | solution.py:31
  64.7 0.1 copy.82
  64.8 0.1 copy.80
  64.9 0.3 fusion.55
  65.1 0.0 copy-start.3
  65.2 13.8 %all_gather.6 = f32[128,2,8,64]{0,3,1,2:T(8,128)S(1)} all-gather(f32[128,2,2,64]{0,3,1,2:T(8,128)S(1)} %copy.84), channel_id=1, replica_groups=mesh['slab'=8,'grp'=4] {'grp'}, dimensions={2}, use_global_device_ids=true | all-gather | bytes 655360 | tf_op jit(solution)/shard_map/all_gather | solution.py:49
  79.0 0.1 copy.87
  79.1 0.0 copy-done.3
  79.1 0.4 fusion.43
  79.5 0.0 copy-start.5
  79.6 0.1 copy.89
  79.7 12.8 %all-gather = f32[1,256,1,4,32]{4,3,2,0,1:T(4,128)S(1)} all-gather(f32[1,64,1,4,32]{4,3,2,0,1:T(4,128)S(1)} %copy.89), channel_id=2, replica_groups=mesh['slab'=8,'grp'=4] {'grp'}, dimensions={1}, use_global_device_ids=true | all-gather | bytes 163840 | tf_op jit(solution)/shard_map/all_gather | solution.py:51
  92.4 0.2 copy.108
  92.7 0.0 copy-done.5
  92.7 0.0 copy-start.1
  92.8 2.2 %fusion.14 = f32[1,4,8,5,128]{4,2,3,1,0:T(8,128)S(1)} fusion(f32[3,3,3,256,128]{4,3,2,1,0:T(8,128)} %param.19, f32[256,1,4,1,7,2]{0,4,5,2,3,1:T(8,128)S(1)} %slice.118, f32[256,1,4,1,8,5]{0,4,5,2,3,1:T(8,128)S(1)} %copy.92, pred[8,5]{0,1:T(8,128)(4,1)S(1)} %copy-done.5), kind=kOutput, calls=%fused_computation.16 | convolution fusion | flops 236122112 | bytes 1482792 | tf_op jit(solution)/shard_map/conv_general_dilated | solution.py:31
  94.9 2.0 %fusion.17 = f32[1,4,8,5,128]{4,2,3,1,0:T(8,128)S(1)} fusion(f32[3,3,3,256,128]{4,3,2,1,0:T(8,128)} %param.19, f32[256,1,4,1,7,2]{0,4,5,2,3,1:T(8,128)S(1)} %slice.118, f32[256,1,4,1,8,5]{0,4,5,2,3,1:T(8,128)S(1)} %copy.92, pred[8,5]{0,1:T(8,128)(4,1)S(1)} %copy-done.5), kind=kOutput, calls=%fused_computation.17 | convolution fusion | flops 236122112 | bytes 1482792 | tf_op jit(solution)/shard_map/conv_general_dilated | solution.py:31
  97.0 7.3 %collective-permute-start.8 = (f32[128,1,4,32]{0,2,3,1:T(4,128)S(1)}, f32[128,1,4,32]{0,2,3,1:T(4,128)S(1)}, u32[]{:S(2)}, u32[]{:S(2)}) collective-permute-start(f32[128,1,4,32]{0,2,3,1:T(4,128)S(1)} %slice_bitcast_fusion.1), channel_id=1, source_target_pairs={{0,4},{4,8},{8,12},{12,16},{16,20},{20,24},{24,28},{1,5},{5,9},{9,... | collective-permute-start | bytes 196616 | tf_op jit(solution)/shard_map/ppermute | solution.py:27
  104.4 1.9 %collective-permute-start.9 = (f32[128,1,4,32]{0,2,3,1:T(4,128)S(1)}, f32[128,1,4,32]{0,2,3,1:T(4,128)S(1)}, u32[]{:S(2)}, u32[]{:S(2)}) collective-permute-start(f32[128,1,4,32]{0,2,3,1:T(4,128)S(1)} %slice_bitcast_fusion), channel_id=1, source_target_pairs={{4,0},{8,4},{12,8},{16,12},{20,16},{24,20},{28,24},{5,1},{9,5},{13... | collective-permute-start | bytes 196616 | tf_op jit(solution)/shard_map/ppermute | solution.py:27
  106.3 2.0 %convolution_select_fusion.1 = f32[1,4,8,5,128]{4,2,3,1,0:T(8,128)S(1)} fusion(f32[3,3,3,256,128]{4,3,2,1,0:T(8,128)S(1)} %copy-done.1, f32[256,1,4,1,7,2]{0,4,5,2,3,1:T(8,128)S(1)} %slice.118, f32[256,1,4,1,8,5]{0,4,5,2,3,1:T(8,128)S(1)} %copy.92, pred[8,5]{0,1:T(8,128)(4,1)S(1)} %copy-done.5), kind=kOutput, calls=%fused_computation.18 | convolution fusion | flops 236122112 | bytes 3842088 | tf_op jit(solution)/shard_map/conv_general_dilated | solution.py:31
  108.3 0.0 collective-permute-done.8
  108.4 2.5 %collective-permute-done.9 = f32[128,1,4,32]{0,2,3,1:T(4,128)S(1)} collective-permute-done((f32[128,1,4,32]{0,2,3,1:T(4,128)S(1)}, f32[128,1,4,32]{0,2,3,1:T(4,128)S(1)}, u32[]{:S(2)}, u32[]{:S(2)}) %collective-permute-start.9) | collective-permute-done | bytes 65568 | tf_op jit(solution)/shard_map/ppermute | solution.py:27
  110.9 0.3 fusion.67
  111.2 0.7 copy.99
  (30 shorter events, 0.5 us)
Async XLA Ops:
  0.0 62.5 %copy-start = (f32[3,3,3,128,128]{4,3,2,1,0:T(8,128)S(1)}, f32[3,3,3,128,128]{4,3,2,1,0:T(8,128)}, u32[]{:S(2)}) copy-start(f32[3,3,3,128,128]{4,3,2,1,0:T(8,128)} %param.17) | copy-start | bytes 5308420
  0.0 6.8 %copy-start.2 = (f32[64,4,4,128]{3,2,1,0:T(4,128)S(1)}, f32[64,4,4,128]{3,2,1,0:T(4,128)}, u32[]{:S(2)}) copy-start(f32[64,4,4,128]{3,2,1,0:T(4,128)} %param.14) | copy-start | bytes 1572868
  1.2 5.6 %collective-permute-start = (f32[64,1,4,128]{3,0,2,1:T(8,128)S(1)}, f32[64,1,4,128]{3,0,2,1:T(8,128)S(1)}, u32[]{:S(2)}, u32[]{:S(2)}) collective-permute-start(f32[64,1,4,128]{3,0,2,1:T(8,128)S(1)} %copy.117), channel_id=1, source_target_pairs={{0,4},{4,8},{8,12},{12,16},{16,20},{20,24},{24,28},{1,5},{5,9},{9,... | collective-permute-start | bytes 393224 | tf_op jit(solution)/shard_map/ppermute | solution.py:15
  4.9 7.2 %collective-permute-start.1 = (f32[64,1,4,128]{3,0,2,1:T(8,128)S(1)}, f32[64,1,4,128]{3,0,2,1:T(8,128)S(1)}, u32[]{:S(2)}, u32[]{:S(2)}) collective-permute-start(f32[64,1,4,128]{3,0,2,1:T(8,128)S(1)} %copy.118), channel_id=1, source_target_pairs={{4,0},{8,4},{12,8},{16,12},{20,16},{24,20},{28,24},{5,1},{9,5},{13... | collective-permute-start | bytes 393224 | tf_op jit(solution)/shard_map/ppermute | solution.py:17
  12.1 6.3 %collective-permute-start.2 = (f32[64,6,1,128]{3,0,2,1:T(8,128)S(1)}, f32[64,6,1,128]{3,0,2,1:T(8,128)S(1)}, u32[]{:S(2)}, u32[]{:S(2)}) collective-permute-start(f32[64,6,1,128]{3,0,2,1:T(8,128)S(1)} %get-tuple-element.45), channel_id=1, source_target_pairs={{0,1},{1,2},{2,3},{4,5},{5,6},{6,7},{8,9},{9,10},{10,11},{12,13},{... | collective-permute-start | bytes 589832 | tf_op jit(solution)/shard_map/ppermute | solution.py:15
  15.3 7.1 %collective-permute-start.3 = (f32[64,6,1,128]{3,0,2,1:T(8,128)S(1)}, f32[64,6,1,128]{3,0,2,1:T(8,128)S(1)}, u32[]{:S(2)}, u32[]{:S(2)}) collective-permute-start(f32[64,6,1,128]{3,0,2,1:T(8,128)S(1)} %get-tuple-element.46), channel_id=1, source_target_pairs={{1,0},{2,1},{3,2},{5,4},{6,5},{7,6},{9,8},{10,9},{11,10},{13,12},{... | collective-permute-start | bytes 589832 | tf_op jit(solution)/shard_map/ppermute | solution.py:17
  30.2 1.2 %copy-start.7 = (f32[3,3,3,64,64]{4,3,2,1,0:T(8,128)S(1)}, f32[3,3,3,64,64]{4,3,2,1,0:T(8,128)}, u32[]{:S(2)}) copy-start(f32[3,3,3,64,64]{4,3,2,1,0:T(8,128)} %param.15) | copy-start | bytes 1327108
  30.2 1.2 %copy-start.8 = (pred[8,17]{0,1:T(8,128)(4,1)S(1)}, pred[8,17]{0,1:T(8,128)(4,1)}, u32[]{:S(2)}) copy-start(pred[8,17]{0,1:T(8,128)(4,1)} %constant.216) | copy-start | bytes 412
  40.6 1.0 copy-start.4
  42.2 6.1 %collective-permute-start.4 = (f32[128,1,2,64]{0,3,2,1:T(8,128)S(1)}, f32[128,1,2,64]{0,3,2,1:T(8,128)S(1)}, u32[]{:S(2)}, u32[]{:S(2)}) collective-permute-start(f32[128,1,2,64]{0,3,2,1:T(8,128)S(1)} %get-tuple-element.53), channel_id=1, source_target_pairs={{0,4},{4,8},{8,12},{12,16},{16,20},{20,24},{24,28},{1,5},{5,9},{9,... | collective-permute-start | bytes 196616 | tf_op jit(solution)/shard_map/ppermute | solution.py:15
  46.4 6.5 %collective-permute-start.5 = (f32[128,1,2,64]{0,3,2,1:T(8,128)S(1)}, f32[128,1,2,64]{0,3,2,1:T(8,128)S(1)}, u32[]{:S(2)}, u32[]{:S(2)}) collective-permute-start(f32[128,1,2,64]{0,3,2,1:T(8,128)S(1)} %get-tuple-element.54), channel_id=1, source_target_pairs={{4,0},{8,4},{12,8},{16,12},{20,16},{24,20},{28,24},{5,1},{9,5},{13... | collective-permute-start | bytes 196616 | tf_op jit(solution)/shard_map/ppermute | solution.py:17
  52.9 5.1 %collective-permute-start.6 = (f32[128,4,1,64]{0,3,2,1:T(8,128)S(1)}, f32[128,4,1,64]{0,3,2,1:T(8,128)S(1)}, u32[]{:S(2)}, u32[]{:S(2)}) collective-permute-start(f32[128,4,1,64]{0,3,2,1:T(8,128)S(1)} %get-tuple-element.49), channel_id=1, source_target_pairs={{0,1},{1,2},{2,3},{4,5},{5,6},{6,7},{8,9},{9,10},{10,11},{12,13},{... | collective-permute-start | bytes 393224 | tf_op jit(solution)/shard_map/ppermute | solution.py:15
  56.2 5.7 %collective-permute-start.7 = (f32[128,4,1,64]{0,3,2,1:T(8,128)S(1)}, f32[128,4,1,64]{0,3,2,1:T(8,128)S(1)}, u32[]{:S(2)}, u32[]{:S(2)}) collective-permute-start(f32[128,4,1,64]{0,3,2,1:T(8,128)S(1)} %get-tuple-element.50), channel_id=1, source_target_pairs={{1,0},{2,1},{3,2},{5,4},{6,5},{7,6},{9,8},{10,9},{11,10},{13,12},{... | collective-permute-start | bytes 393224 | tf_op jit(solution)/shard_map/ppermute | solution.py:17
  62.3 0.7 copy-start.6
  65.1 14.0 %copy-start.3 = (f32[2,2,2,128,64]{3,4,2,1,0:T(8,128)S(1)}, f32[2,2,2,128,64]{3,4,2,1,0:T(8,128)}, u32[]{:S(2)}) copy-start(f32[2,2,2,128,64]{3,4,2,1,0:T(8,128)} %param.18) | copy-start | bytes 786436
  79.5 13.2 %copy-start.5 = (pred[8,5]{0,1:T(8,128)(4,1)S(1)}, pred[8,5]{0,1:T(8,128)(4,1)}, u32[]{:S(2)}) copy-start(pred[8,5]{0,1:T(8,128)(4,1)} %constant.213) | copy-start | bytes 124
  92.7 13.6 %copy-start.1 = (f32[3,3,3,256,128]{4,3,2,1,0:T(8,128)S(1)}, f32[3,3,3,256,128]{4,3,2,1,0:T(8,128)}, u32[]{:S(2)}) copy-start(f32[3,3,3,256,128]{4,3,2,1,0:T(8,128)} %param.19) | copy-start | bytes 10616836
  97.0 11.3 %collective-permute-start.8 = (f32[128,1,4,32]{0,2,3,1:T(4,128)S(1)}, f32[128,1,4,32]{0,2,3,1:T(4,128)S(1)}, u32[]{:S(2)}, u32[]{:S(2)}) collective-permute-start(f32[128,1,4,32]{0,2,3,1:T(4,128)S(1)} %slice_bitcast_fusion.1), channel_id=1, source_target_pairs={{0,4},{4,8},{8,12},{12,16},{16,20},{20,24},{24,28},{1,5},{5,9},{9,... | collective-permute-start | bytes 196616 | tf_op jit(solution)/shard_map/ppermute | solution.py:27
  104.4 6.5 %collective-permute-start.9 = (f32[128,1,4,32]{0,2,3,1:T(4,128)S(1)}, f32[128,1,4,32]{0,2,3,1:T(4,128)S(1)}, u32[]{:S(2)}, u32[]{:S(2)}) collective-permute-start(f32[128,1,4,32]{0,2,3,1:T(4,128)S(1)} %slice_bitcast_fusion), channel_id=1, source_target_pairs={{4,0},{8,4},{12,8},{16,12},{20,16},{24,20},{28,24},{5,1},{9,5},{13... | collective-permute-start | bytes 196616 | tf_op jit(solution)/shard_map/ppermute | solution.py:27
where the time goes:
time: 112 us
  starting transfers between devices  29.9 us (27%)
  blocking collectives  26.6 us (24%)
  waiting for transfers between devices  22.4 us (20%)
  matrix products  17.7 us (16%)
  local copies, waits for them, and re-layouts  14 us (12%)
    conv_general_dilated x7, matrix products, convolve(): lax.conv_general_dilated(field[None], kernel, (stride, stride, stride), p...  17.7 us
    ppermute x4, waiting for transfers between devices, padded_2(): lax.ppermute(head, axis, [((i + 1) % count, i) for i in range(ends)])  17.5 us
    ppermute x4, starting transfers between devices, padded_2(): lax.ppermute(tail, axis, [(i, (i + 1) % count) for i in range(ends)])  14.3 us
    all_gather x1, blocking collectives, per_device(): gathered = lax.all_gather(level_two, 'grp', axis=2, tiled=True)  13.8 us
    all_gather x1, blocking collectives, per_device(): coarse = lax.all_gather(shares, 'grp', axis=0, tiled=True)  12.8 us
    ppermute x2, starting transfers between devices, from_behind(): return lax.ppermute(shard, axis, pairs)  9.24 us
    unnamed x25, local copies, waits for them, and re-layouts  6.57 us
    ppermute x4, starting transfers between devices, padded_2(): lax.ppermute(head, axis, [((i + 1) % count, i) for i in range(ends)])  6.43 us
  transfers between devices with their start and end apart: 10, of which 7 were waited for; matrix products, arithmetic and copies ran while one was open for 2% of the time, Pallas kernels for 0%

commit v1 on v0

--- a/solution.py
+++ b/solution.py
@@ -46,7 +46,7 @@
     level_two = convolve(level_one, down_first, 2, valid)
     padded_two = padded_2(level_two, (("slab", 1), ("grp", 2)), 1)
     level_two = jax.nn.gelu(convolve(padded_two, conv_middle, 1, sideways), approximate=False)
-    gathered = lax.all_gather(level_two, "grp", axis=2, tiled=True)
+    gathered = jnp.concatenate(lax.all_gather(level_two, "grp"), axis=2)
     shares = convolve(gathered, down_second, 2, valid)
     coarse = lax.all_gather(shares, "grp", axis=0, tiled=True)
     planar = ((0, 0), (1, 1), (1, 1))

time: 112 us -> 113 us (level)
  no operation moved by 1% of the time
where the time goes in v1:
time: 113 us
  starting transfers between devices  29.9 us (26%)
  blocking collectives  26.5 us (23%)
  waiting for transfers between devices  22.4 us (20%)
  matrix products  18 us (16%)
  local copies, waits for them, and re-layouts  14.7 us (13%)
    conv_general_dilated x7, matrix products, convolve(): lax.conv_general_dilated(field[None], kernel, (stride, stride, stride), p...  18 us
    ppermute x4, waiting for transfers between devices, padded_2(): lax.ppermute(head, axis, [((i + 1) % count, i) for i in range(ends)])  17.5 us
    ppermute x4, starting transfers between devices, padded_2(): lax.ppermute(tail, axis, [(i, (i + 1) % count) for i in range(ends)])  14.3 us
    all_gather x1, blocking collectives, per_device(): gathered = jnp.concatenate(lax.all_gather(level_two, 'grp'), axis=2)  13.7 us
    all_gather x1, blocking collectives, per_device(): coarse = lax.all_gather(shares, 'grp', axis=0, tiled=True)  12.8 us
    ppermute x2, starting transfers between devices, from_behind(): return lax.ppermute(shard, axis, pairs)  9.25 us
    unnamed x25, local copies, waits for them, and re-layouts  7.37 us
    ppermute x4, starting transfers between devices, padded_2(): lax.ppermute(head, axis, [((i + 1) % count, i) for i in range(ends)])  6.43 us
  transfers between devices with their start and end apart: 10, of which 7 were waited for; matrix products, arithmetic and copies ran while one was open for 2% of the time, Pallas kernels for 0%

profile of v1, /device:TPU:3, one launch (start us, length us, event | category | flops | bytes accessed | tf_op | source)
XLA Modules:
  0.0 112.5 jit_solution(2615987414007153775)
XLA Ops:
  0.0 0.0 copy-start
  0.0 0.0 copy-start.2
  0.0 1.1 %fusion.101 = (f32[64,1,4,128]{3,2,1,0:T(4,128)S(1)}, f32[64,1,4,128]{3,2,1,0:T(4,128)S(1)}) fusion(f32[64,4,4,128]{3,2,1,0:T(4,128)} %param.14), kind=kLoop, calls=%fused_computation.131 | loop fusion | bytes 524288 | tf_op jit(solution)/shard_map/slice | solution.py:11
  1.2 3.7 %collective-permute-start = (f32[64,1,4,128]{3,0,2,1:T(8,128)S(1)}, f32[64,1,4,128]{3,0,2,1:T(8,128)S(1)}, u32[]{:S(2)}, u32[]{:S(2)}) collective-permute-start(f32[64,1,4,128]{3,0,2,1:T(8,128)S(1)} %copy.71), channel_id=1, source_target_pairs={{0,4},{4,8},{8,12},{12,16},{16,20},{20,24},{24,28},{1,5},{5,9},{9,... | collective-permute-start | bytes 393224 | tf_op jit(solution)/shard_map/ppermute | solution.py:15
  4.9 1.9 %collective-permute-start.1 = (f32[64,1,4,128]{3,0,2,1:T(8,128)S(1)}, f32[64,1,4,128]{3,0,2,1:T(8,128)S(1)}, u32[]{:S(2)}, u32[]{:S(2)}) collective-permute-start(f32[64,1,4,128]{3,0,2,1:T(8,128)S(1)} %copy.72), channel_id=1, source_target_pairs={{4,0},{8,4},{12,8},{16,12},{20,16},{24,20},{28,24},{5,1},{9,5},{13... | collective-permute-start | bytes 393224 | tf_op jit(solution)/shard_map/ppermute | solution.py:17
  6.8 0.0 collective-permute-done
  6.8 0.0 copy-done.2
  6.8 0.2 constant_dynamic-update-slice_fusion.1
  7.0 5.1 %collective-permute-done.1 = f32[64,1,4,128]{3,0,2,1:T(8,128)S(1)} collective-permute-done((f32[64,1,4,128]{3,0,2,1:T(8,128)S(1)}, f32[64,1,4,128]{3,0,2,1:T(8,128)S(1)}, u32[]{:S(2)}, u32[]{:S(2)}) %collective-permute-start.1) | collective-permute-done | bytes 131104 | tf_op jit(solution)/shard_map/ppermute | solution.py:17
  12.1 3.2 %collective-permute-start.2 = (f32[64,6,1,128]{3,0,2,1:T(8,128)S(1)}, f32[64,6,1,128]{3,0,2,1:T(8,128)S(1)}, u32[]{:S(2)}, u32[]{:S(2)}) collective-permute-start(f32[64,6,1,128]{3,0,2,1:T(8,128)S(1)} %get-tuple-element.45), channel_id=1, source_target_pairs={{0,1},{1,2},{2,3},{4,5},{5,6},{6,7},{8,9},{9,10},{10,11},{12,13},{... | collective-permute-start | bytes 589832 | tf_op jit(solution)/shard_map/ppermute | solution.py:15
  15.3 1.3 %collective-permute-start.3 = (f32[64,6,1,128]{3,0,2,1:T(8,128)S(1)}, f32[64,6,1,128]{3,0,2,1:T(8,128)S(1)}, u32[]{:S(2)}, u32[]{:S(2)}) collective-permute-start(f32[64,6,1,128]{3,0,2,1:T(8,128)S(1)} %get-tuple-element.46), channel_id=1, source_target_pairs={{1,0},{2,1},{3,2},{5,4},{6,5},{7,6},{9,8},{10,9},{11,10},{13,12},{... | collective-permute-start | bytes 589832 | tf_op jit(solution)/shard_map/ppermute | solution.py:17
  16.6 1.7 %collective-permute-done.2 = f32[64,6,1,128]{3,0,2,1:T(8,128)S(1)} collective-permute-done((f32[64,6,1,128]{3,0,2,1:T(8,128)S(1)}, f32[64,6,1,128]{3,0,2,1:T(8,128)S(1)}, u32[]{:S(2)}, u32[]{:S(2)}) %collective-permute-start.2) | collective-permute-done | bytes 196640 | tf_op jit(solution)/shard_map/ppermute | solution.py:15
  18.4 4.1 %collective-permute-done.3 = f32[64,6,1,128]{3,0,2,1:T(8,128)S(1)} collective-permute-done((f32[64,6,1,128]{3,0,2,1:T(8,128)S(1)}, f32[64,6,1,128]{3,0,2,1:T(8,128)S(1)}, u32[]{:S(2)}, u32[]{:S(2)}) %collective-permute-start.3) | collective-permute-done | bytes 196640 | tf_op jit(solution)/shard_map/ppermute | solution.py:17
  22.5 0.1 maximum_bitcast_fusion
  22.6 4.3 %copy.66 = f32[64,6,6,1,128]{0,3,4,2,1:T(1,128)} copy(f32[64,6,6,1,128]{4,0,2,1,3:T(8,128)S(1)} %maximum_bitcast_fusion) | data formatting | bytes 2359296
  26.9 3.4 %pad.6.clone = f32[64,6,6,1,136]{0,3,4,2,1:T(1,128)S(1)} pad(f32[64,6,6,1,128]{0,3,4,2,1:T(1,128)} %copy.66, f32[]{:T(128)} %constant.74.clone.1), padding=0_0x0_0x0_0x0_0x1_7 | pad | bytes 2433028 | tf_op jit(solution)/shard_map/broadcast_in_dim | solution.py:32
  30.2 0.0 copy-start.6
  30.2 0.0 copy-start.7
  30.2 0.2 copy.38
  30.5 0.9 copy-done.6
  31.4 0.0 copy-done.7
  31.4 8.9 %fusion.22 = f32[4,4,8,17,64]{4,2,3,1,0:T(8,128)S(1)} fusion(f32[3,3,3,64,64]{4,3,2,1,0:T(8,128)S(1)} %copy-done.6, f32[64,6,6,1,7,2]{0,4,5,2,1,3:T(8,128)S(1)} %slice.106, f32[64,6,6,1,8,17]{0,4,5,2,1,3:T(8,128)S(1)} %copy.38, pred[8,17]{0,1:T(8,128)(4,1)S(1)} %copy-done.7), kind=kOutput, calls=%fused_computation.21 | convolution fusion | flops 1454131200 | bytes 2381960 | tf_op jit(solution)/shard_map/conv_general_dilated | solution.py:31
  40.3 0.3 copy.39
  40.6 0.1 slice.107
  40.7 0.0 copy-start.4
  40.7 0.8 copy.42
  41.5 0.1 copy-done.4
  41.6 0.6 fusion.24
  42.3 4.2 %collective-permute-start.4 = (f32[128,1,2,64]{0,3,2,1:T(8,128)S(1)}, f32[128,1,2,64]{0,3,2,1:T(8,128)S(1)}, u32[]{:S(2)}, u32[]{:S(2)}) collective-permute-start(f32[128,1,2,64]{0,3,2,1:T(8,128)S(1)} %get-tuple-element.51), channel_id=1, source_target_pairs={{0,4},{4,8},{8,12},{12,16},{16,20},{20,24},{24,28},{1,5},{5,9},{9,... | collective-permute-start | bytes 196616 | tf_op jit(solution)/shard_map/ppermute | solution.py:15
  46.4 1.9 %collective-permute-start.5 = (f32[128,1,2,64]{0,3,2,1:T(8,128)S(1)}, f32[128,1,2,64]{0,3,2,1:T(8,128)S(1)}, u32[]{:S(2)}, u32[]{:S(2)}) collective-permute-start(f32[128,1,2,64]{0,3,2,1:T(8,128)S(1)} %get-tuple-element.52), channel_id=1, source_target_pairs={{4,0},{8,4},{12,8},{16,12},{20,16},{24,20},{28,24},{5,1},{9,5},{13... | collective-permute-start | bytes 196616 | tf_op jit(solution)/shard_map/ppermute | solution.py:17
  48.4 0.0 collective-permute-done.4
  48.4 4.5 %collective-permute-done.5 = f32[128,1,2,64]{0,3,2,1:T(8,128)S(1)} collective-permute-done((f32[128,1,2,64]{0,3,2,1:T(8,128)S(1)}, f32[128,1,2,64]{0,3,2,1:T(8,128)S(1)}, u32[]{:S(2)}, u32[]{:S(2)}) %collective-permute-start.5) | collective-permute-done | bytes 65568 | tf_op jit(solution)/shard_map/ppermute | solution.py:17
  53.0 3.2 %collective-permute-start.6 = (f32[128,4,1,64]{0,3,2,1:T(8,128)S(1)}, f32[128,4,1,64]{0,3,2,1:T(8,128)S(1)}, u32[]{:S(2)}, u32[]{:S(2)}) collective-permute-start(f32[128,4,1,64]{0,3,2,1:T(8,128)S(1)} %get-tuple-element.49), channel_id=1, source_target_pairs={{0,1},{1,2},{2,3},{4,5},{5,6},{6,7},{8,9},{9,10},{10,11},{12,13},{... | collective-permute-start | bytes 393224 | tf_op jit(solution)/shard_map/ppermute | solution.py:15
  56.2 1.3 %collective-permute-start.7 = (f32[128,4,1,64]{0,3,2,1:T(8,128)S(1)}, f32[128,4,1,64]{0,3,2,1:T(8,128)S(1)}, u32[]{:S(2)}, u32[]{:S(2)}) collective-permute-start(f32[128,4,1,64]{0,3,2,1:T(8,128)S(1)} %get-tuple-element.50), channel_id=1, source_target_pairs={{1,0},{2,1},{3,2},{5,4},{6,5},{7,6},{9,8},{10,9},{11,10},{13,12},{... | collective-permute-start | bytes 393224 | tf_op jit(solution)/shard_map/ppermute | solution.py:17
  57.5 0.6 collective-permute-done.6
  58.1 3.8 %collective-permute-done.7 = f32[128,4,1,64]{0,3,2,1:T(8,128)S(1)} collective-permute-done((f32[128,4,1,64]{0,3,2,1:T(8,128)S(1)}, f32[128,4,1,64]{0,3,2,1:T(8,128)S(1)}, u32[]{:S(2)}, u32[]{:S(2)}) %collective-permute-start.7) | collective-permute-done | bytes 131104 | tf_op jit(solution)/shard_map/ppermute | solution.py:17
  61.9 0.3 copy.67
  62.3 0.0 copy-start.8
  62.3 0.1 pad.9.clone
  62.5 0.0 copy-done
  62.5 0.5 copy-done.8
  63.0 2.0 %fusion.55 = f32[2,2,8,9,128]{4,2,3,1,0:T(8,128)S(1)} fusion(f32[3,3,3,128,128]{4,3,2,1,0:T(8,128)S(1)} %copy-done, f32[128,4,4,1,7,2]{0,4,5,2,1,3:T(8,128)S(1)} %slice.113, f32[128,4,4,1,8,9]{0,4,5,2,1,3:T(8,128)S(1)} %copy.46, pred[8,9]{0,1:T(8,128)(4,1)S(1)} %copy-done.8), kind=kOutput, calls=%fused_computation.67 | convolution fusion | flops 767348736 | bytes 2621512 | tf_op jit(solution)/shard_map/conv_general_dilated | solution.py:31
  65.0 0.1 copy.47
  65.1 13.7 %all_gather.7 = f32[4,128,2,2,64]{1,4,3,2,0:T(8,128)S(1)} all-gather(f32[1,128,2,2,64]{1,4,3,2,0:T(8,128)S(1)} %copy.48), channel_id=1, replica_groups=mesh['slab'=8,'grp'=4] {'grp'}, dimensions={0}, use_global_device_ids=true | all-gather | bytes 655360 | tf_op jit(solution)/shard_map/all_gather | solution.py:49
  78.8 0.0 copy-start.3
  78.8 0.1 copy.51
  79.0 0.8 copy-done.3
  79.7 0.4 fusion.43
  80.1 0.0 copy-start.5
  80.2 0.1 copy.53
  80.3 12.8 %all-gather = f32[1,256,1,4,32]{4,3,2,0,1:T(4,128)S(1)} all-gather(f32[1,64,1,4,32]{4,3,2,0,1:T(4,128)S(1)} %copy.53), channel_id=2, replica_groups=mesh['slab'=8,'grp'=4] {'grp'}, dimensions={1}, use_global_device_ids=true | all-gather | bytes 163840 | tf_op jit(solution)/shard_map/all_gather | solution.py:51
  93.0 0.2 copy.68
  93.3 0.0 copy-done.5
  93.3 0.0 copy-start.1
  93.4 2.2 %fusion.14 = f32[1,4,8,5,128]{4,2,3,1,0:T(8,128)S(1)} fusion(f32[3,3,3,256,128]{4,3,2,1,0:T(8,128)} %param.19, f32[256,1,4,1,7,2]{0,4,5,2,3,1:T(8,128)S(1)} %slice.116, f32[256,1,4,1,8,5]{0,4,5,2,3,1:T(8,128)S(1)} %copy.56, pred[8,5]{0,1:T(8,128)(4,1)S(1)} %copy-done.5), kind=kOutput, calls=%fused_computation.16 | convolution fusion | flops 236122112 | bytes 1482792 | tf_op jit(solution)/shard_map/conv_general_dilated | solution.py:31
  95.5 2.0 %fusion.17 = f32[1,4,8,5,128]{4,2,3,1,0:T(8,128)S(1)} fusion(f32[3,3,3,256,128]{4,3,2,1,0:T(8,128)} %param.19, f32[256,1,4,1,7,2]{0,4,5,2,3,1:T(8,128)S(1)} %slice.116, f32[256,1,4,1,8,5]{0,4,5,2,3,1:T(8,128)S(1)} %copy.56, pred[8,5]{0,1:T(8,128)(4,1)S(1)} %copy-done.5), kind=kOutput, calls=%fused_computation.17 | convolution fusion | flops 236122112 | bytes 1482792 | tf_op jit(solution)/shard_map/conv_general_dilated | solution.py:31
  97.6 7.3 %collective-permute-start.8 = (f32[128,1,4,32]{0,2,3,1:T(4,128)S(1)}, f32[128,1,4,32]{0,2,3,1:T(4,128)S(1)}, u32[]{:S(2)}, u32[]{:S(2)}) collective-permute-start(f32[128,1,4,32]{0,2,3,1:T(4,128)S(1)} %slice_bitcast_fusion.2), channel_id=1, source_target_pairs={{0,4},{4,8},{8,12},{12,16},{16,20},{20,24},{24,28},{1,5},{5,9},{9,... | collective-permute-start | bytes 196616 | tf_op jit(solution)/shard_map/ppermute | solution.py:27
  105.0 1.9 %collective-permute-start.9 = (f32[128,1,4,32]{0,2,3,1:T(4,128)S(1)}, f32[128,1,4,32]{0,2,3,1:T(4,128)S(1)}, u32[]{:S(2)}, u32[]{:S(2)}) collective-permute-start(f32[128,1,4,32]{0,2,3,1:T(4,128)S(1)} %slice_bitcast_fusion.1), channel_id=1, source_target_pairs={{4,0},{8,4},{12,8},{16,12},{20,16},{24,20},{28,24},{5,1},{9,5},{13... | collective-permute-start | bytes 196616 | tf_op jit(solution)/shard_map/ppermute | solution.py:27
  106.9 0.0 copy-done.1
  106.9 2.0 %convolution_select_fusion.1 = f32[1,4,8,5,128]{4,2,3,1,0:T(8,128)S(1)} fusion(f32[3,3,3,256,128]{4,3,2,1,0:T(8,128)S(1)} %copy-done.1, f32[256,1,4,1,7,2]{0,4,5,2,3,1:T(8,128)S(1)} %slice.116, f32[256,1,4,1,8,5]{0,4,5,2,3,1:T(8,128)S(1)} %copy.56, pred[8,5]{0,1:T(8,128)(4,1)S(1)} %copy-done.5), kind=kOutput, calls=%fused_computation.18 | convolution fusion | flops 236122112 | bytes 3842088 | tf_op jit(solution)/shard_map/conv_general_dilated | solution.py:31
  109.0 0.0 collective-permute-done.8
  109.0 2.5 %collective-permute-done.9 = f32[128,1,4,32]{0,2,3,1:T(4,128)S(1)} collective-permute-done((f32[128,1,4,32]{0,2,3,1:T(4,128)S(1)}, f32[128,1,4,32]{0,2,3,1:T(4,128)S(1)}, u32[]{:S(2)}, u32[]{:S(2)}) %collective-permute-start.9) | collective-permute-done | bytes 65568 | tf_op jit(solution)/shard_map/ppermute | solution.py:27
  111.5 0.3 fusion.71
  111.8 0.7 copy.63
  (28 shorter events, 0.5 us)
Async XLA Ops:
  0.0 62.5 %copy-start = (f32[3,3,3,128,128]{4,3,2,1,0:T(8,128)S(1)}, f32[3,3,3,128,128]{4,3,2,1,0:T(8,128)}, u32[]{:S(2)}) copy-start(f32[3,3,3,128,128]{4,3,2,1,0:T(8,128)} %param.17) | copy-start | bytes 5308420
  0.0 6.8 %copy-start.2 = (f32[64,4,4,128]{3,2,1,0:T(4,128)S(1)}, f32[64,4,4,128]{3,2,1,0:T(4,128)}, u32[]{:S(2)}) copy-start(f32[64,4,4,128]{3,2,1,0:T(4,128)} %param.14) | copy-start | bytes 1572868
  1.2 5.6 %collective-permute-start = (f32[64,1,4,128]{3,0,2,1:T(8,128)S(1)}, f32[64,1,4,128]{3,0,2,1:T(8,128)S(1)}, u32[]{:S(2)}, u32[]{:S(2)}) collective-permute-start(f32[64,1,4,128]{3,0,2,1:T(8,128)S(1)} %copy.71), channel_id=1, source_target_pairs={{0,4},{4,8},{8,12},{12,16},{16,20},{20,24},{24,28},{1,5},{5,9},{9,... | collective-permute-start | bytes 393224 | tf_op jit(solution)/shard_map/ppermute | solution.py:15
  4.9 7.2 %collective-permute-start.1 = (f32[64,1,4,128]{3,0,2,1:T(8,128)S(1)}, f32[64,1,4,128]{3,0,2,1:T(8,128)S(1)}, u32[]{:S(2)}, u32[]{:S(2)}) collective-permute-start(f32[64,1,4,128]{3,0,2,1:T(8,128)S(1)} %copy.72), channel_id=1, source_target_pairs={{4,0},{8,4},{12,8},{16,12},{20,16},{24,20},{28,24},{5,1},{9,5},{13... | collective-permute-start | bytes 393224 | tf_op jit(solution)/shard_map/ppermute | solution.py:17
  12.1 6.3 %collective-permute-start.2 = (f32[64,6,1,128]{3,0,2,1:T(8,128)S(1)}, f32[64,6,1,128]{3,0,2,1:T(8,128)S(1)}, u32[]{:S(2)}, u32[]{:S(2)}) collective-permute-start(f32[64,6,1,128]{3,0,2,1:T(8,128)S(1)} %get-tuple-element.45), channel_id=1, source_target_pairs={{0,1},{1,2},{2,3},{4,5},{5,6},{6,7},{8,9},{9,10},{10,11},{12,13},{... | collective-permute-start | bytes 589832 | tf_op jit(solution)/shard_map/ppermute | solution.py:15
  15.3 7.1 %collective-permute-start.3 = (f32[64,6,1,128]{3,0,2,1:T(8,128)S(1)}, f32[64,6,1,128]{3,0,2,1:T(8,128)S(1)}, u32[]{:S(2)}, u32[]{:S(2)}) collective-permute-start(f32[64,6,1,128]{3,0,2,1:T(8,128)S(1)} %get-tuple-element.46), channel_id=1, source_target_pairs={{1,0},{2,1},{3,2},{5,4},{6,5},{7,6},{9,8},{10,9},{11,10},{13,12},{... | collective-permute-start | bytes 589832 | tf_op jit(solution)/shard_map/ppermute | solution.py:17
  30.2 1.2 %copy-start.6 = (f32[3,3,3,64,64]{4,3,2,1,0:T(8,128)S(1)}, f32[3,3,3,64,64]{4,3,2,1,0:T(8,128)}, u32[]{:S(2)}) copy-start(f32[3,3,3,64,64]{4,3,2,1,0:T(8,128)} %param.15) | copy-start | bytes 1327108
  30.2 1.2 %copy-start.7 = (pred[8,17]{0,1:T(8,128)(4,1)S(1)}, pred[8,17]{0,1:T(8,128)(4,1)}, u32[]{:S(2)}) copy-start(pred[8,17]{0,1:T(8,128)(4,1)} %constant.216) | copy-start | bytes 412
  40.7 1.0 copy-start.4
  42.3 6.1 %collective-permute-start.4 = (f32[128,1,2,64]{0,3,2,1:T(8,128)S(1)}, f32[128,1,2,64]{0,3,2,1:T(8,128)S(1)}, u32[]{:S(2)}, u32[]{:S(2)}) collective-permute-start(f32[128,1,2,64]{0,3,2,1:T(8,128)S(1)} %get-tuple-element.51), channel_id=1, source_target_pairs={{0,4},{4,8},{8,12},{12,16},{16,20},{20,24},{24,28},{1,5},{5,9},{9,... | collective-permute-start | bytes 196616 | tf_op jit(solution)/shard_map/ppermute | solution.py:15
  46.4 6.5 %collective-permute-start.5 = (f32[128,1,2,64]{0,3,2,1:T(8,128)S(1)}, f32[128,1,2,64]{0,3,2,1:T(8,128)S(1)}, u32[]{:S(2)}, u32[]{:S(2)}) collective-permute-start(f32[128,1,2,64]{0,3,2,1:T(8,128)S(1)} %get-tuple-element.52), channel_id=1, source_target_pairs={{4,0},{8,4},{12,8},{16,12},{20,16},{24,20},{28,24},{5,1},{9,5},{13... | collective-permute-start | bytes 196616 | tf_op jit(solution)/shard_map/ppermute | solution.py:17
  53.0 5.1 %collective-permute-start.6 = (f32[128,4,1,64]{0,3,2,1:T(8,128)S(1)}, f32[128,4,1,64]{0,3,2,1:T(8,128)S(1)}, u32[]{:S(2)}, u32[]{:S(2)}) collective-permute-start(f32[128,4,1,64]{0,3,2,1:T(8,128)S(1)} %get-tuple-element.49), channel_id=1, source_target_pairs={{0,1},{1,2},{2,3},{4,5},{5,6},{6,7},{8,9},{9,10},{10,11},{12,13},{... | collective-permute-start | bytes 393224 | tf_op jit(solution)/shard_map/ppermute | solution.py:15
  56.2 5.7 %collective-permute-start.7 = (f32[128,4,1,64]{0,3,2,1:T(8,128)S(1)}, f32[128,4,1,64]{0,3,2,1:T(8,128)S(1)}, u32[]{:S(2)}, u32[]{:S(2)}) collective-permute-start(f32[128,4,1,64]{0,3,2,1:T(8,128)S(1)} %get-tuple-element.50), channel_id=1, source_target_pairs={{1,0},{2,1},{3,2},{5,4},{6,5},{7,6},{9,8},{10,9},{11,10},{13,12},{... | collective-permute-start | bytes 393224 | tf_op jit(solution)/shard_map/ppermute | solution.py:17
  62.3 0.7 copy-start.8
  78.8 1.0 copy-start.3
  80.1 13.2 %copy-start.5 = (pred[8,5]{0,1:T(8,128)(4,1)S(1)}, pred[8,5]{0,1:T(8,128)(4,1)}, u32[]{:S(2)}) copy-start(pred[8,5]{0,1:T(8,128)(4,1)} %constant.213) | copy-start | bytes 124
  93.3 13.6 %copy-start.1 = (f32[3,3,3,256,128]{4,3,2,1,0:T(8,128)S(1)}, f32[3,3,3,256,128]{4,3,2,1,0:T(8,128)}, u32[]{:S(2)}) copy-start(f32[3,3,3,256,128]{4,3,2,1,0:T(8,128)} %param.19) | copy-start | bytes 10616836
  97.6 11.3 %collective-permute-start.8 = (f32[128,1,4,32]{0,2,3,1:T(4,128)S(1)}, f32[128,1,4,32]{0,2,3,1:T(4,128)S(1)}, u32[]{:S(2)}, u32[]{:S(2)}) collective-permute-start(f32[128,1,4,32]{0,2,3,1:T(4,128)S(1)} %slice_bitcast_fusion.2), channel_id=1, source_target_pairs={{0,4},{4,8},{8,12},{12,16},{16,20},{20,24},{24,28},{1,5},{5,9},{9,... | collective-permute-start | bytes 196616 | tf_op jit(solution)/shard_map/ppermute | solution.py:27
  105.0 6.5 %collective-permute-start.9 = (f32[128,1,4,32]{0,2,3,1:T(4,128)S(1)}, f32[128,1,4,32]{0,2,3,1:T(4,128)S(1)}, u32[]{:S(2)}, u32[]{:S(2)}) collective-permute-start(f32[128,1,4,32]{0,2,3,1:T(4,128)S(1)} %slice_bitcast_fusion.1), channel_id=1, source_target_pairs={{4,0},{8,4},{12,8},{16,12},{20,16},{24,20},{28,24},{5,1},{9,5},{13... | collective-permute-start | bytes 196616 | tf_op jit(solution)/shard_map/ppermute | solution.py:27
